TPU v7x, 32 devices: a whole 2x2x4 slice. The times are simulated.
32 devices in a mesh: dp: 2 (over y), seq: 8 (over z, x), head: 2 (over core).
Axes of the slice: x: 2, y: 2, z: 4, core: 2. Of those that a mesh axis runs over, the one named last changes fastest.
Arguments:
- tokens: bfloat16 [2, 2, 1024, 2048], P(None, 'dp', 'seq'), may hold values from -6 to 6
- norm_gain: float32 [2048], replicated, may hold values from 0.5 to 1.5
- w_gate_in: bfloat16 [2048, 4096], P(('dp', 'seq'), 'head'), may hold values from -0.125 to 0.125
- w_x_in: bfloat16 [2048, 4096], P(('dp', 'seq'), 'head'), may hold values from -0.125 to 0.125
- w_bc_in: bfloat16 [2048, 256], P(('dp', 'seq')), may hold values from -0.125 to 0.125
- w_dt_in: bfloat16 [2048, 64], P(('dp', 'seq'), 'head'), may hold values from -0.0625 to 0.0625
- conv_x_w: float32 [4, 4096], P(None, 'head'), may hold values from -3 to 3
- conv_x_b: float32 [4096], P('head'), may hold values from -3 to 3
- conv_bc_w: float32 [4, 256], replicated, may hold values from -3 to 3
- conv_bc_b: float32 [256], replicated, may hold values from -3 to 3
- dt_bias: float32 [64], P('head'), may hold values from -7 to -2
- a_log: float32 [64], P('head'), may hold values from 0 to 1.5
- d_skip: float32 [64], P('head'), may hold values from 0.5 to 1.5
- gate_gain: float32 [4096], P('head'), may hold values from 0.5 to 1.5
- w_out: bfloat16 [4096, 2048], P('head', ('dp', 'seq')), may hold values from -0.09375 to 0.09375
- prefix_len: int32 [2, 2], P(None, 'dp'), may hold values from 102 to 1024, as said below
- cotangent: bfloat16 [2, 2, 1024, 2048], P(None, 'dp', 'seq'), may hold values from -6 to 6
Outputs:
- result: bfloat16 [2, 2, 1024, 2048], P(None, 'dp', 'seq')
- grad_tokens: float32 [2, 2, 1024, 2048], P(None, 'dp', 'seq')
- grad_norm_gain: float32 [2048], replicated
- grad_w_gate_in: float32 [2048, 4096], P(('dp', 'seq'), 'head')
- grad_w_x_in: float32 [2048, 4096], P(('dp', 'seq'), 'head')
- grad_w_bc_in: float32 [2048, 256], P(('dp', 'seq'))
- grad_w_dt_in: float32 [2048, 64], P(('dp', 'seq'), 'head')
- grad_conv_x_w: float32 [4, 4096], P(None, 'head')
- grad_conv_x_b: float32 [4096], P('head')
- grad_conv_bc_w: float32 [4, 256], replicated
- grad_conv_bc_b: float32 [256], replicated
- grad_dt_bias: float32 [64], P('head')
- grad_a_log: float32 [64], P('head')
- grad_d_skip: float32 [64], P('head')
- grad_gate_gain: float32 [4096], P('head')
- grad_w_out: float32 [4096, 2048], P('head', ('dp', 'seq'))
Inputs may be any that keep to these rules, and one draw needn't show every extreme that they name: Tokens before a sequence's prefix_len mix both ways; some sequence has exactly 1024 and some exactly 102.
All inputs are finite; a program needn't handle non-finite values.
Results may differ from a plain program's by a relative error of at most 0.012.
Values may be sent and summed in bfloat16 or wider, within the bound.
A program may use at most 256 MiB of HBM per device.

v0:
```python
import jax
import jax.numpy as jnp
from jax import lax
from jax.sharding import PartitionSpec as P

EPSILON = 1e-05
HIGHEST = lax.Precision.HIGHEST
BF16 = jnp.bfloat16
F32 = jnp.float32
CHUNK = 128


def dot_f32(a, b):
    return jnp.dot(a, b, preferred_element_type=F32)


def causal_conv(signal, kernel, bias):
    margin = kernel.shape[0] - 1
    length = signal.shape[1]
    padded = jnp.pad(signal, ((0, 0), (margin, 0), (0, 0)))
    summed = bias + jnp.zeros_like(signal)
    for offset in range(kernel.shape[0]):
        summed = summed + kernel[offset] * padded[:, offset : offset + length]
    return summed


def mixer(
    prefix, inner, bc, dt_raw, conv_x_w, conv_x_b, conv_bc_w, conv_bc_b, dt_bias, a_log, d_skip
):
    seqs, length, width = inner.shape
    heads = dt_raw.shape[-1]
    state = bc.shape[-1] // 2
    chunk = CHUNK
    count = length // chunk
    values = jax.nn.silu(causal_conv(inner, conv_x_w, conv_x_b))
    active = jax.nn.silu(causal_conv(bc, conv_bc_w, conv_bc_b))
    values = values.reshape(seqs, count, chunk, heads, width // heads)
    b_in = active[..., :state].reshape(seqs, count, chunk, state)
    c_out = active[..., state:].reshape(seqs, count, chunk, state)
    dt = jax.nn.softplus(dt_raw + dt_bias).reshape(seqs, count, chunk, heads)
    cum = jnp.cumsum(dt * -jnp.exp(a_log), axis=2)
    end = cum[:, :, -1:, :]
    places = jnp.arange(length, dtype=jnp.int32).reshape(count, chunk)
    inside = (places[None] < prefix[:, None, None])[..., None]
    weighted = values * dt[..., None]
    ends_state = jnp.einsum(
        "skth,skthp,sktn->skhpn", jnp.exp(end - cum), weighted, b_in, precision=HIGHEST
    )
    back_state = jnp.einsum(
        "skth,skthp,sktn->skhpn",
        jnp.where(inside, jnp.exp(cum), 0.0),
        weighted,
        b_in,
        precision=HIGHEST,
    )
    decay = jnp.exp(end[:, :, 0])[..., None, None]
    zero = jnp.zeros_like(ends_state[:, 0])
    state_in, back_in = ([zero], [zero])
    for k in range(count - 1):
        state_in.append(state_in[-1] * decay[:, k] + ends_state[:, k])
        back_in.append(back_in[-1] * decay[:, count - 1 - k] + back_state[:, count - 1 - k])
    state_in = jnp.stack(state_in, axis=1)
    back_in = jnp.stack(back_in[::-1], axis=1)
    scores = jnp.einsum("sktn,skun->sktu", c_out, b_in, precision=HIGHEST)
    spread = cum[:, :, :, None, :] - cum[:, :, None, :, :]
    behind = (places[:, :, None] >= places[:, None, :])[None, ..., None]
    ahead = (
        (places[:, :, None] < places[:, None, :])[None]
        & (places[None, :, None, :] < prefix[:, None, None, None])
    )[..., None]
    masked = jnp.where(behind, jnp.exp(jnp.where(behind, spread, 0.0)), 0.0) + jnp.where(
        ahead, jnp.exp(jnp.where(ahead, -spread, 0.0)), 0.0
    )
    out = jnp.einsum("sktuh,skuhp->skthp", scores[..., None] * masked, weighted, precision=HIGHEST)
    out = out + jnp.exp(cum)[..., None] * jnp.einsum(
        "sktn,skhpn->skthp", c_out, state_in, precision=HIGHEST
    )
    out = out + jnp.exp(end - cum)[..., None] * jnp.einsum(
        "sktn,skhpn->skthp", c_out, back_in, precision=HIGHEST
    )
    out = out + d_skip[:, None] * values
    return out.reshape(seqs, length, width)


def body(
    tokens,
    norm_gain,
    w_gate_in,
    w_x_in,
    w_bc_in,
    w_dt_in,
    conv_x_w,
    conv_x_b,
    conv_bc_w,
    conv_bc_b,
    dt_bias,
    a_log,
    d_skip,
    gate_gain,
    w_out,
    prefix_len,
    cotangent,
):
    dp, sq, hd = (lax.axis_size("dp"), lax.axis_size("seq"), lax.axis_size("head"))
    me_seq, me_head = (lax.axis_index("seq"), lax.axis_index("head"))
    micro, seqs, span, model = tokens.shape
    group = micro * seqs
    length = span * sq
    rows_here = group * span
    own_rows = rows_here // hd
    half = w_x_in.shape[1]
    width = half // sq
    heads = w_dt_in.shape[1] // sq
    full_inner = half * hd
    prefix = prefix_len.reshape(group)
    everyone = ("seq", "head")

    def mine(x):
        return lax.dynamic_slice_in_dim(
            x.reshape(rows_here, model), me_head * own_rows, own_rows, 0
        )

    def to_sequences(x):
        return x.reshape(sq, group, span, -1).transpose(1, 0, 2, 3).reshape(group, length, -1)

    def from_sequences(x):
        return x.reshape(group, sq, span, -1).transpose(1, 0, 2, 3).reshape(sq * rows_here, -1)

    def rms(x, gain):
        return x * lax.rsqrt(jnp.mean(x * x, axis=-1, keepdims=True) + EPSILON) * gain

    my_tokens = mine(tokens).astype(F32)
    my_cot = mine(cotangent)
    normed_own = rms(my_tokens, norm_gain).astype(BF16)
    normed = lax.all_gather(normed_own, everyone, axis=0, tiled=True)

    def columns(w):
        return lax.all_gather(
            lax.all_to_all(w, "seq", split_axis=1, concat_axis=0, tiled=True),
            "dp",
            axis=0,
            tiled=True,
        )

    wg = columns(w_gate_in)
    wx = columns(w_x_in)
    wd = lax.dynamic_slice_in_dim(
        lax.all_gather(w_dt_in, ("dp", "seq"), axis=0, tiled=True), me_seq * heads, heads, 1
    )
    wb = lax.all_gather(w_bc_in, ("dp", "seq"), axis=0, tiled=True)
    wo = lax.all_gather(
        lax.all_to_all(w_out, "seq", split_axis=0, concat_axis=1, tiled=True),
        "dp",
        axis=1,
        tiled=True,
    )
    cot = lax.all_gather(my_cot, everyone, axis=0, tiled=True)

    def part(x, size, axis):
        return lax.dynamic_slice_in_dim(x, me_seq * size, size, axis)

    cxw, cxb = (part(conv_x_w, width, 1), part(conv_x_b, width, 0))
    dtb, alog, dsk = (part(dt_bias, heads, 0), part(a_log, heads, 0), part(d_skip, heads, 0))
    gain = part(gate_gain, width, 0)

    def project(w):
        return to_sequences(dot_f32(normed, w).astype(BF16)).astype(F32)

    gate, inner, bc, dt_raw = (project(wg), project(wx), project(wb), project(wd))
    mixed, pull = jax.vjp(
        lambda *a: mixer(prefix, *a),
        inner,
        bc,
        dt_raw,
        cxw,
        cxb,
        conv_bc_w,
        conv_bc_b,
        dtb,
        alog,
        dsk,
    )
    sig = jax.nn.sigmoid(gate)
    act = gate * sig
    gated = mixed * act
    grad_scaled = to_sequences(jnp.einsum("rd,kd->rk", cot, wo, preferred_element_type=F32))
    gs = grad_scaled * gain
    sums = lax.psum(
        jnp.stack([jnp.sum(gated * gated, axis=-1), jnp.sum(gs * gated, axis=-1)]), everyone
    )
    scale = lax.rsqrt(sums[0][..., None] / full_inner + EPSILON)
    unit = gated * scale
    scaled = from_sequences((unit * gain).astype(BF16))
    branch = lax.psum_scatter(
        dot_f32(scaled, wo).astype(BF16), everyone, scatter_dimension=0, tiled=True
    )
    result_own = (my_tokens + branch.astype(F32)).astype(BF16)
    grad_gain = jnp.sum(grad_scaled * unit, axis=(0, 1))
    grad_wo = jnp.einsum("rk,rd->kd", scaled, cot, preferred_element_type=F32)
    grad_gated = gs * scale - gated * (scale * scale * scale * (sums[1][..., None] / full_inner))
    grad_mixed = grad_gated * act
    grad_gate = grad_gated * mixed * (sig * (1.0 + gate * (1.0 - sig)))
    d_inner, d_bc, d_dt, d_cxw, d_cxb, d_cbw, d_cbb, d_dtb, d_alog, d_dsk = pull(grad_mixed)
    gg = from_sequences(grad_gate.astype(BF16))
    gx = from_sequences(d_inner.astype(BF16))
    gd = from_sequences(d_dt.astype(BF16))
    gb_own = lax.psum_scatter(
        from_sequences(d_bc), everyone, scatter_dimension=0, tiled=True
    ).astype(BF16)

    def inward(g, w):
        return jnp.einsum("rc,kc->rk", g, w, preferred_element_type=F32)

    def weight_grad(n, g):
        return jnp.einsum("rk,rc->kc", n, g, preferred_element_type=F32)

    part_normed = inward(gg, wg) + inward(gx, wx) + inward(gd, wd)
    grad_normed = lax.psum_scatter(
        part_normed.astype(BF16), everyone, scatter_dimension=0, tiled=True
    ).astype(F32) + inward(gb_own, wb)
    _, pull_norm = jax.vjp(rms, my_tokens, norm_gain)
    grad_rows, grad_norm = pull_norm(grad_normed)
    grad_own = my_cot.astype(F32) + grad_rows

    def home(g):
        return lax.all_to_all(
            lax.psum_scatter(g.astype(BF16), "dp", scatter_dimension=0, tiled=True),
            "seq",
            split_axis=0,
            concat_axis=1,
            tiled=True,
        ).astype(F32)

    g_gate, g_x = (home(weight_grad(normed, gg)), home(weight_grad(normed, gx)))
    g_dt = lax.all_to_all(
        lax.psum_scatter(weight_grad(normed, gd), "dp", scatter_dimension=0, tiled=True),
        "seq",
        split_axis=0,
        concat_axis=1,
        tiled=True,
    )
    g_bc = lax.psum_scatter(
        lax.psum(weight_grad(normed_own, gb_own), "head"),
        ("dp", "seq"),
        scatter_dimension=0,
        tiled=True,
    )
    g_out = lax.all_to_all(
        lax.psum_scatter(grad_wo.astype(BF16), "dp", scatter_dimension=1, tiled=True),
        "seq",
        split_axis=1,
        concat_axis=0,
        tiled=True,
    ).astype(F32)

    def whole(x):
        return lax.all_gather(x, "head", axis=0, tiled=True).reshape(micro, seqs, span, model)

    small = lax.psum((d_cxw, d_cxb, d_dtb, d_alog, d_dsk, grad_gain), "dp")
    small = [lax.all_gather(a, "seq", axis=a.ndim - 1, tiled=True) for a in small]
    grad_norm, d_cbw, d_cbb = lax.psum((grad_norm, d_cbw, d_cbb), ("dp", "seq", "head"))
    return (
        whole(result_own),
        whole(grad_own),
        grad_norm,
        g_gate,
        g_x,
        g_bc,
        g_dt,
        small[0],
        small[1],
        d_cbw,
        d_cbb,
        small[2],
        small[3],
        small[4],
        small[5],
        g_out,
    )


def solution(mesh):
    rows = P(("dp", "seq"), "head")
    tok = P(None, "dp", "seq", None)
    return jax.shard_map(
        body,
        mesh=mesh,
        in_specs=(
            tok,
            P(),
            rows,
            rows,
            P(("dp", "seq"), None),
            rows,
            P(None, "head"),
            P("head"),
            P(),
            P(),
            P("head"),
            P("head"),
            P("head"),
            P("head"),
            P("head", ("dp", "seq")),
            P(None, "dp"),
            tok,
        ),
        out_specs=(
            tok,
            tok,
            P(),
            rows,
            rows,
            P(("dp", "seq"), None),
            rows,
            P(None, "head"),
            P("head"),
            P(),
            P(),
            P("head"),
            P("head"),
            P("head"),
            P("head"),
            P("head", ("dp", "seq")),
        ),
        check_vma=False,
    )
```

profile of v0, /device:TPU:14, one launch (start us, length us, event | category | flops | bytes accessed | tf_op | source)
XLA Modules:
  0.0 1105.0 jit_solution(2029383470495228353)
XLA Ops:
  12.0 27.5 %all_to_all.115 = bf16[128,8,256]{0,2,1:T(8,128)(2,1)S(1)} all-to-all(bf16[128,8,256]{0,2,1:T(8,128)(2,1)S(1)} %bitcast.572), channel_id=1, replica_groups=mesh['dp'=2,'seq'=8,'head'=2] {'seq'}, dimensions={1} | all-to-all | bytes 1048576 | tf_op jit(solution)/shard_map/all_to_all | solution.py:139
  41.4 28.8 %all_to_all.116 = bf16[8,256,128]{2,1,0:T(8,128)(2,1)S(1)} all-to-all(bf16[8,256,128]{2,1,0:T(8,128)(2,1)S(1)} %bitcast.582), channel_id=1, replica_groups=mesh['dp'=2,'seq'=8,'head'=2] {'seq'}, dimensions={0} | all-to-all | bytes 1048576 | tf_op jit(solution)/shard_map/all_to_all | solution.py:152
  73.2 8.3 all-to-all-start.1
  83.4 42.2 %all_gather.47 = bf16[2048,32]{0,1:T(8,128)(2,1)S(1)} all-gather(bf16[128,32]{0,1:T(8,128)(2,1)S(1)} %copy-done.97), channel_id=1, replica_groups=mesh['dp'=2,'seq'=8,'head'=2] {'dp','seq'}, dimensions={0}, use_global_device_ids=true | all-gather | bytes 139264 | tf_op jit(solution)/shard_map/all_gather | solution.py:148
  129.6 5.6 fusion.19
  135.8 47.9 %fusion.184 = f32[2,8,128,4]{3,1,2,0:T(8,128)S(1)} fusion(f32[2,8,128,4]{3,1,2,0:T(8,128)S(1)} %copy.524), kind=kOutput, calls=%fused_computation.362 | output fusion | flops 1040384 | bytes 65536 | tf_op jit(solution)/shard_map/jvp(jit(cumsum))/reduce_window_sum | solution.py:41
  184.5 6.0 convolution_convert_fusion.6
  192.2 6.0 convolution_convert_fusion.5
  198.6 12.3 %all-gather.21.cloned.1.call-done = bf16[256,2048]{0,1:T(8,128)(2,1)} async-done(((bf16[256,1024]{0,1:T(8,128)(2,1)}), bf16[256,2048]{0,1:T(8,128)(2,1)}) %all-gather.21.cloned.1.call-update) | async-done | bytes 1048592 | tf_op jit(solution)/shard_map/all_gather | solution.py:151
  210.9 76.9 %all-gather.19.cloned.1.call-done = bf16[2048,2048]{1,0:T(8,128)(2,1)} async-done(((bf16[128,2048]{1,0:T(8,128)(2,1)}), bf16[2048,2048]{1,0:T(8,128)(2,1)}) %all-gather.19.cloned.1.call-update) | async-done | bytes 8388624 | tf_op jit(solution)/shard_map/all_gather | solution.py:157
  287.8 7.3 fusion.188
  295.1 3.0 copy.565
  298.3 11.7 %all-gather.17.cloned.1.call-done = bf16[2048,256]{1,0:T(8,128)(2,1)} async-done(((bf16[1024,256]{1,0:T(8,128)(2,1)}), bf16[2048,256]{1,0:T(8,128)(2,1)}) %all-gather.17.cloned.1.call-update) | async-done | bytes 1048592 | tf_op jit(solution)/shard_map/all_gather | solution.py:138
  310.0 6.0 convolution_convert_fusion.4
  318.4 2.9 copy.560
  321.4 6.9 fusion.44
  328.3 5.1 reshape.593
  333.3 4.9 copy.522
  338.3 2.6 fusion.43
  356.7 10.7 multiply_reduce_fusion.16
  367.4 3.1 copy.559
  370.5 2.6 multiply_reduce_fusion.15
  373.1 48.8 %psum.77 = f32[2,2,1024]{2,1,0:T(2,128)S(1)} all-reduce(f32[2,2,1024]{2,1,0:T(2,128)S(1)} %pad_maximum_fusion), channel_id=1, replica_groups=mesh['dp'=2,'seq'=8,'head'=2] {'seq','head'}, use_global_device_ids=true, to_apply=%region_4.5 | all-reduce | flops 4096 | bytes 32768 | tf_op jit(solution)/shard_map/psum | solution.py:188
  423.2 5.9 multiply_reduce_fusion.13
  429.2 3.6 fusion.72
  436.4 4.5 fusion.69
  440.9 3.3 fusion.111
  447.5 4.5 fusion.78
  452.0 3.2 fusion.51
  455.2 12.5 %fusion.12 = (f32[2,8,128,128]{3,2,1,0:T(8,128)}, f32[2,8,128,128,4]{3,2,4,1,0:T(8,128)}) fusion(f32[2,8,128,4]{2,3,1,0:T(4,128)S(1)} %copy-done.72, pred[2,8,128,128]{3,2,1,0:T(8,128)(4,1)S(1)} %copy-done.51, pred[8,128,128]{2,1,0:T(8,128)(4,1)S(1)} %copy-done.56, f32[2,8,128,128]{3,2,1,0:T(8,128)S(1)} %copy-done.41, ...), kind=kOutput, calls=%fused_computation.18 | convolution fusion | flops 824442880 | bytes 10944512 | tf_op jit(solution)/shard_map/transpose(jvp(sktuh,skuhp->skthp))/dot_general | solution.py:74
  467.7 4.6 fusion.90
  474.5 4.1 fusion.175
  478.7 9.8 multiply_reduce_fusion
  491.9 47.3 %fusion.185 = f32[2,8,128,4]{3,1,2,0:T(8,128)S(1)} fusion(f32[2,8,128,4]{3,1,2,0:T(8,128)S(1)} %copy.609), kind=kOutput, calls=%fused_computation.363 | output fusion | flops 1040384 | bytes 65536 | tf_op jit(solution)/shard_map/transpose(jvp(jit(cumsum)))/reduce_window_sum | solution.py:41
  539.8 4.8 copy.658
  544.6 5.8 reshape.594
  550.5 3.4 multiply_reduce_fusion.10
  566.2 8.1 fusion.156
  574.3 3.2 multiply_reduce_fusion.2
  577.5 8.4 fusion.189
  585.9 16.1 %add_convert_fusion = bf16[2048,2048]{1,0:T(8,128)(2,1)} fusion(f32[2048,2048]{1,0:T(8,128)} %fusion.156, f32[2048,2048]{1,0:T(8,128)} %fusion.189, bf16[2048,256]{1,0:T(8,128)(2,1)S(1)} %bitcast.562, bf16[2048,256]{1,0:T(8,128)(2,1)S(1)} %copy-done.36), kind=kOutput, calls=%fused_computation | convolution fusion | flops 2160066560 | bytes 44040192 | tf_op jit(solution)/shard_map/rc,kc->rk/dot_general | solution.py:212
  603.5 5.6 convolution_convert_fusion
  609.2 6.9 fusion.190
  616.4 6.9 convolution_convert_fusion.3
  623.4 7.0 convolution_convert_fusion.2
  630.4 6.9 convolution_convert_fusion.1
  637.5 2.8 fusion.150
  640.3 105.5 %reduce-scatter.13.cloned.1.call-done = bf16[128,2048]{1,0:T(8,128)(2,1)} async-done(((bf16[2048,2048]{1,0:T(8,128)(2,1)}), bf16[128,2048]{1,0:T(8,128)(2,1)}) %reduce-scatter.13.cloned.1.call-update) | async-done | bytes 524304 | tf_op jit(solution)/shard_map/reduce_scatter | solution.py:218
  747.9 106.9 %reduce-scatter.11.cloned.1.call-done = bf16[128,2048]{1,0:T(8,128)(2,1)} async-done(((bf16[2048,2048]{1,0:T(8,128)(2,1)}), bf16[128,2048]{1,0:T(8,128)(2,1)}) %reduce-scatter.11.cloned.1.call-update) | async-done | bytes 524304 | tf_op jit(solution)/shard_map/reduce_scatter | solution.py:194
  854.8 2.6 fusion.97
  857.4 19.1 %reduce-scatter.25.cloned.1.call-done = f32[1024,4]{1,0:T(8,128)} async-done(((f32[2048,4]{1,0:T(8,128)}), f32[1024,4]{1,0:T(8,128)}) %reduce-scatter.25.cloned.1.call-update) | async-done | bytes 16400
  877.7 10.1 all_to_all.117
  887.8 11.9 %reduce-scatter.17.cloned.1.call-done = bf16[1024,256]{1,0:T(8,128)(2,1)} async-done(((bf16[2048,256]{1,0:T(8,128)(2,1)}), bf16[1024,256]{1,0:T(8,128)(2,1)}) %reduce-scatter.17.cloned.1.call-update) | async-done | bytes 524304 | tf_op jit(solution)/shard_map/reduce_scatter | solution.py:227
  899.7 6.0 all-to-all-start.3
  906.3 16.5 %reduce-scatter.19.cloned.1.call-done = bf16[1024,256]{1,0:T(8,128)(2,1)} async-done(((bf16[2048,256]{1,0:T(8,128)(2,1)}), bf16[1024,256]{1,0:T(8,128)(2,1)}) %reduce-scatter.19.cloned.1.call-update) | async-done | bytes 524304 | tf_op jit(solution)/shard_map/reduce_scatter | solution.py:227
  922.8 6.0 all-to-all-start.4
  930.3 15.1 %reduce-scatter.21.cloned.1.call-done = bf16[256,1024]{1,0:T(8,128)(2,1)} async-done(((bf16[256,2048]{1,0:T(8,128)(2,1)}), bf16[256,1024]{1,0:T(8,128)(2,1)}) %reduce-scatter.21.cloned.1.call-update) | async-done | bytes 524304 | tf_op jit(solution)/shard_map/reduce_scatter | solution.py:249
  947.3 6.0 all-to-all-start.6
  953.5 5.0 all-reduce.54
  958.5 19.4 %all-gather = f32[8,1,256]{2,1,0:T(1,128)S(1)} all-gather(f32[1,1,256]{2,1,0:T(1,128)S(1)} %bitcast.633), channel_id=1, replica_groups=mesh['dp'=2,'seq'=8,'head'=2] {'seq'}, dimensions={0}, use_global_device_ids=true | all-gather | bytes 9216 | tf_op jit(solution)/shard_map/all_gather | solution.py:260
  977.9 15.5 %all-gather.1 = f32[8,1,256]{2,1,0:T(1,128)S(1)} all-gather(f32[1,1,256]{2,1,0:T(1,128)S(1)} %bitcast.632), channel_id=1, replica_groups=mesh['dp'=2,'seq'=8,'head'=2] {'seq'}, dimensions={0}, use_global_device_ids=true | all-gather | bytes 9216 | tf_op jit(solution)/shard_map/all_gather | solution.py:260
  993.4 27.9 %all_gather.54 = f32[4,2048]{1,0:T(4,128)S(1)} all-gather(f32[4,256]{1,0:T(4,128)S(1)} %get-tuple-element.164), channel_id=1, replica_groups=mesh['dp'=2,'seq'=8,'head'=2] {'seq'}, dimensions={1}, use_global_device_ids=true | all-gather | bytes 36864 | tf_op jit(solution)/shard_map/all_gather | solution.py:260
  1021.9 22.0 %all-reduce.53 = (f32[32]{0:T(128)}, f32[32]{0:T(128)}, f32[32]{0:T(128)}) all-reduce(f32[32]{0:T(128)S(1)} %dynamic-update-slice, f32[32]{0:T(128)S(1)} %dynamic-update-slice.1, f32[32]{0:T(128)S(1)} %dynamic-update-slice.2), channel_id=1, replica_groups=mesh['dp'=2,'seq'=8,'head'=2] {'seq'}, use_global_device_ids=true, to_apply=%add.49 | all-reduce | flops 96 | bytes 768
  1047.4 43.9 %all-reduce.52 = (f32[2048]{0:T(1024)}, f32[4,256]{1,0:T(4,128)}, f32[256]{0:T(256)}) all-reduce(f32[2048]{0:T(1024)S(1)} %get-tuple-element.135, f32[4,256]{1,0:T(4,128)S(1)} %pad_add_fusion.10, f32[256]{0:T(256)S(1)} %get-tuple-element.131), channel_id=1, replica_groups=mesh['dp'=2,'seq'=8,'head'=2] {'dp','seq','head'}, use_global_device_ids=true, to_apply=%region_33.34 | all-reduce | flops 3328 | bytes 26624 | tf_op jit(solution)/shard_map/psum | solution.py:261
  (405 shorter events, 82.8 us)
Async XLA Ops:
  7.2 122.4 %all-gather.11.cloned.1.call-start = ((), (), s32[]{:S(2)}) async-start(), calls=%async_computation.15 | async-start | bytes 8912896 | tf_op jit(solution)/shard_map/all_gather | solution.py:135
  11.7 29.7 %copy-start.47 = (bf16[2048,128]{1,0:T(8,128)(2,1)S(1)}, bf16[2048,128]{1,0:T(8,128)(2,1)}, u32[]{:S(2)}) copy-start(bf16[2048,128]{1,0:T(8,128)(2,1)} %param.31) | copy-start | bytes 1572868
  11.7 172.8 %all-gather.13.cloned.1.call-start = ((), (), s32[]{:S(2)}) async-start(), calls=%async_computation.16 | async-start | bytes 1572864 | tf_op jit(solution)/shard_map/all_gather | solution.py:138
  39.5 31.8 %copy-start.43 = (bf16[2,1,128,2048]{3,2,1,0:T(8,128)(2,1)S(1)}, bf16[2,1,128,2048]{3,2,1,0:T(8,128)(2,1)}, u32[]{:S(2)}) copy-start(bf16[2,1,128,2048]{3,2,1,0:T(8,128)(2,1)} %param.33) | copy-start | bytes 3145732
  40.6 151.7 %all-gather.15.cloned.1.call-start = ((), (), s32[]{:S(2)}) async-start(), calls=%async_computation.17 | async-start | bytes 1114112 | tf_op jit(solution)/shard_map/all_gather | solution.py:150
  41.3 169.6 %all-gather.21.cloned.1.call-start = ((), (), s32[]{:S(2)}) async-start(), calls=%async_computation.20 | async-start | bytes 1572864 | tf_op jit(solution)/shard_map/all_gather | solution.py:151
  41.4 30.9 %copy-start.48 = (bf16[128,2048]{1,0:T(8,128)(2,1)S(1)}, bf16[128,2048]{1,0:T(8,128)(2,1)}, u32[]{:S(2)}) copy-start(bf16[128,2048]{1,0:T(8,128)(2,1)} %param.19) | copy-start | bytes 1572868
  71.2 12.1 %copy-start.97 = (bf16[128,32]{0,1:T(8,128)(2,1)S(1)}, bf16[128,32]{0,1:T(8,128)(2,1)}, u32[]{:S(2)}) copy-start(bf16[128,32]{0,1:T(8,128)(2,1)} %param.22) | copy-start | bytes 24580
  71.3 54.3 %copy-start.112 = (f32[32]{0:T(128)S(1)}, f32[32]{0:T(128)}, u32[]{:S(2)}) copy-start(f32[32]{0:T(128)} %param.27) | copy-start | bytes 388
  71.3 54.4 %copy-start.113 = (f32[32]{0:T(128)S(1)}, f32[32]{0:T(128)}, u32[]{:S(2)}) copy-start(f32[32]{0:T(128)} %param.29) | copy-start | bytes 388
  71.3 56.6 %copy-start.108 = (s32[2,1]{0,1:T(1,128)S(1)}, s32[2,1]{0,1:T(1,128)}, u32[]{:S(2)}) copy-start(s32[2,1]{0,1:T(1,128)} %param.32) | copy-start | bytes 28
  71.3 56.7 %copy-start.104 = (f32[4,256]{1,0:T(4,128)S(1)}, f32[4,256]{1,0:T(4,128)}, u32[]{:S(2)}) copy-start(f32[4,256]{1,0:T(4,128)} %param.25) | copy-start | bytes 12292
  71.3 216.5 %all-gather.19.cloned.1.call-start = ((), (), s32[]{:S(2)}) async-start(), calls=%async_computation.19 | async-start | bytes 8912896 | tf_op jit(solution)/shard_map/all_gather | solution.py:157
  73.2 55.2 %all-to-all-start.1 = ((bf16[128,8,256]{0,2,1:T(8,128)(2,1)}), bf16[128,8,256]{0,2,1:T(8,128)(2,1)S(1)}, u32[]{:S(2)}, u32[]{:S(2)}) async-start(bf16[128,8,256]{0,2,1:T(8,128)(2,1)} %bitcast.42), calls=%async_computation.1 | async-start | bytes 1048576 | tf_op jit(solution)/shard_map/all_to_all | solution.py:139
  81.6 228.4 %all-gather.17.cloned.1.call-start = ((), (), s32[]{:S(2)}) async-start(), calls=%async_computation.18 | async-start | bytes 1572864 | tf_op jit(solution)/shard_map/all_gather | solution.py:138
  81.7 53.6 %copy-start.100 = (f32[4]{0:T(128)}, f32[4]{0:T(128)S(1)}, u32[]{:S(2)}) copy-start(f32[4]{0:T(128)S(1)} %fusion.174) | copy-start | bytes 52
  82.6 238.7 %copy-start.81 = (f32[1,256]{1,0:T(1,128)}, f32[1,256]{1,0:T(1,128)S(1)}, u32[]{:S(2)}) copy-start(f32[1,256]{1,0:T(1,128)S(1)} %get-tuple-element.230) | copy-start | bytes 3076
  82.6 238.7 %copy-start.83 = (f32[1,256]{1,0:T(1,128)}, f32[1,256]{1,0:T(1,128)S(1)}, u32[]{:S(2)}) copy-start(f32[1,256]{1,0:T(1,128)S(1)} %get-tuple-element.231) | copy-start | bytes 3076
  82.6 238.7 %copy-start.85 = (f32[1,256]{1,0:T(1,128)}, f32[1,256]{1,0:T(1,128)S(1)}, u32[]{:S(2)}) copy-start(f32[1,256]{1,0:T(1,128)S(1)} %get-tuple-element.232) | copy-start | bytes 3076
  82.6 238.7 %copy-start.87 = (f32[1,256]{1,0:T(1,128)}, f32[1,256]{1,0:T(1,128)S(1)}, u32[]{:S(2)}) copy-start(f32[1,256]{1,0:T(1,128)S(1)} %get-tuple-element.233) | copy-start | bytes 3076
  125.7 230.9 %copy-start.115 = (f32[4]{0:T(128)}, f32[4]{0:T(128)S(1)}, u32[]{:S(2)}) copy-start(f32[4]{0:T(128)S(1)} %dynamic_slice.33) | copy-start | bytes 52
  128.0 70.2 %copy-start.67 = (pred[2,8,128]{2,1,0:T(8,128)(4,1)}, pred[2,8,128]{2,1,0:T(8,128)(4,1)S(1)}, u32[]{:S(2)}) copy-start(pred[2,8,128]{2,1,0:T(8,128)(4,1)S(1)} %broadcast_compare_fusion.2) | copy-start | bytes 6148
  128.0 210.3 %copy-start.89 = (f32[1,256]{1,0:T(1,128)}, f32[1,256]{1,0:T(1,128)S(1)}, u32[]{:S(2)}) copy-start(f32[1,256]{1,0:T(1,128)S(1)} %get-tuple-element.239) | copy-start | bytes 3076
  128.0 210.3 %copy-start.91 = (f32[1,256]{1,0:T(1,128)}, f32[1,256]{1,0:T(1,128)S(1)}, u32[]{:S(2)}) copy-start(f32[1,256]{1,0:T(1,128)S(1)} %get-tuple-element.240) | copy-start | bytes 3076
  128.0 210.3 %copy-start.93 = (f32[1,256]{1,0:T(1,128)}, f32[1,256]{1,0:T(1,128)S(1)}, u32[]{:S(2)}) copy-start(f32[1,256]{1,0:T(1,128)S(1)} %get-tuple-element.241) | copy-start | bytes 3076
  128.0 210.3 %copy-start.95 = (f32[1,256]{1,0:T(1,128)}, f32[1,256]{1,0:T(1,128)S(1)}, u32[]{:S(2)}) copy-start(f32[1,256]{1,0:T(1,128)S(1)} %get-tuple-element.242) | copy-start | bytes 3076
  128.3 228.4 %copy-start.55 = (pred[8,128,128]{2,1,0:T(8,128)(4,1)}, pred[8,128,128]{2,1,0:T(8,128)(4,1)S(1)}, u32[]{:S(2)}) copy-start(pred[8,128,128]{2,1,0:T(8,128)(4,1)S(1)} %get-tuple-element.237) | copy-start | bytes 393220
  128.4 228.2 %copy-start.50 = (pred[2,8,128,128]{3,2,1,0:T(8,128)(4,1)}, pred[2,8,128,128]{3,2,1,0:T(8,128)(4,1)S(1)}, u32[]{:S(2)}) copy-start(pred[2,8,128,128]{3,2,1,0:T(8,128)(4,1)S(1)} %broadcast_and_fusion) | copy-start | bytes 786436
  129.5 508.0 %reduce-scatter.15.cloned.1.call-start = ((), (), s32[]{:S(2)}) async-start(), calls=%async_computation.24 | async-start | bytes 2228224 | tf_op jit(solution)/shard_map/reduce_scatter | solution.py:207
  184.5 172.2 %copy-start.71 = (f32[2,8,128,4]{2,3,1,0:T(4,128)}, f32[2,8,128,4]{2,3,1,0:T(4,128)S(1)}, u32[]{:S(2)}) copy-start(f32[2,8,128,4]{2,3,1,0:T(4,128)S(1)} %copy.525) | copy-start | bytes 98308
  198.4 148.2 %copy-start.59 = (f32[2,8,128,4]{2,3,1,0:T(4,128)}, f32[2,8,128,4]{2,3,1,0:T(4,128)S(1)}, u32[]{:S(2)}) copy-start(f32[2,8,128,4]{2,3,1,0:T(4,128)S(1)} %copy.546) | copy-start | bytes 98308
  198.6 139.7 %copy-start = (f32[8,2,128,256]{3,2,0,1:T(8,128)}, f32[8,2,128,256]{3,2,0,1:T(8,128)S(1)}, u32[]{:S(2)}) copy-start(f32[8,2,128,256]{3,2,0,1:T(8,128)S(1)} %copy.523) | copy-start | bytes 6291460
  298.3 47.0 %copy-start.76 = (f32[2,4]{1,0:T(2,128)}, f32[2,4]{1,0:T(2,128)S(1)}, u32[]{:S(2)}) copy-start(f32[2,4]{1,0:T(2,128)S(1)} %get-tuple-element.150) | copy-start | bytes 100
  298.3 50.6 %copy-start.63 = (f32[2,4]{1,0:T(2,128)}, f32[2,4]{1,0:T(2,128)S(1)}, u32[]{:S(2)}) copy-start(f32[2,4]{1,0:T(2,128)S(1)} %get-tuple-element.154) | copy-start | bytes 100
  298.3 50.6 %copy-start.65 = (f32[2,4]{1,0:T(2,128)}, f32[2,4]{1,0:T(2,128)S(1)}, u32[]{:S(2)}) copy-start(f32[2,4]{1,0:T(2,128)S(1)} %get-tuple-element.157) | copy-start | bytes 100
  298.3 51.1 %copy-start.74 = (f32[2,4]{1,0:T(2,128)}, f32[2,4]{1,0:T(2,128)S(1)}, u32[]{:S(2)}) copy-start(f32[2,4]{1,0:T(2,128)S(1)} %get-tuple-element.151) | copy-start | bytes 100
  341.1 13.2 %copy-start.3 = (f32[2,1024,128]{2,1,0:T(8,128)}, f32[2,1024,128]{2,1,0:T(8,128)S(1)}, u32[]{:S(2)}) copy-start(f32[2,1024,128]{2,1,0:T(8,128)S(1)} %get-tuple-element.221) | copy-start | bytes 3145732
  354.2 13.1 %copy-start.27 = (f32[2,8,128,4,64]{2,4,3,1,0:T(8,128)}, f32[2,8,128,4,64]{2,4,3,1,0:T(8,128)S(1)}, u32[]{:S(2)}) copy-start(f32[2,8,128,4,64]{2,4,3,1,0:T(8,128)S(1)} %fusion.55) | copy-start | bytes 6291460
  455.2 12.5 %copy-start.20 = (f32[2,8,4,64,128]{4,3,2,0,1:T(8,128)S(1)}, f32[2,8,4,64,128]{4,3,2,0,1:T(8,128)}, u32[]{:S(2)}) copy-start(f32[2,8,4,64,128]{4,3,2,0,1:T(8,128)} %copy-done.19) | copy-start | bytes 6291460
  491.5 48.1 %copy-start.53 = (f32[2,8,128,4]{2,3,1,0:T(4,128)S(1)}, f32[2,8,128,4]{2,3,1,0:T(4,128)}, u32[]{:S(2)}) copy-start(f32[2,8,128,4]{2,3,1,0:T(4,128)} %get-tuple-element.137) | copy-start | bytes 98308
  491.5 48.1 %copy-start.101 = (f32[4]{0:T(128)S(1)}, f32[4]{0:T(128)}, u32[]{:S(2)}) copy-start(f32[4]{0:T(128)} %copy-done.100) | copy-start | bytes 52
  491.5 48.1 %copy-start.103 = (f32[4]{0:T(128)S(1)}, f32[4]{0:T(128)}, u32[]{:S(2)}) copy-start(f32[4]{0:T(128)} %copy-done.102) | copy-start | bytes 52
  566.1 179.7 %reduce-scatter.13.cloned.1.call-start = ((), (), s32[]{:S(2)}) async-start(), calls=%async_computation.23 | async-start | bytes 8912896 | tf_op jit(solution)/shard_map/reduce_scatter | solution.py:218
  602.0 252.8 %reduce-scatter.11.cloned.1.call-start = ((), (), s32[]{:S(2)}) async-start(), calls=%async_computation.21 | async-start | bytes 8912896 | tf_op jit(solution)/shard_map/reduce_scatter | solution.py:194
  609.1 267.4 %reduce-scatter.25.cloned.1.call-start = ((), (), s32[]{:S(2)}) async-start(), calls=%async_computation.31 | async-start | bytes 1572864
  616.1 283.6 %reduce-scatter.17.cloned.1.call-start = ((), (), s32[]{:S(2)}) async-start(), calls=%async_computation.26 | async-start | bytes 1572864 | tf_op jit(solution)/shard_map/reduce_scatter | solution.py:227
  623.3 299.5 %reduce-scatter.19.cloned.1.call-start = ((), (), s32[]{:S(2)}) async-start(), calls=%async_computation.27 | async-start | bytes 1572864 | tf_op jit(solution)/shard_map/reduce_scatter | solution.py:227
  630.4 315.0 %reduce-scatter.21.cloned.1.call-start = ((), (), s32[]{:S(2)}) async-start(), calls=%async_computation.28 | async-start | bytes 1572864 | tf_op jit(solution)/shard_map/reduce_scatter | solution.py:249
  637.3 108.5 %copy-start.31 = (bf16[2,1,128,2048]{3,2,1,0:T(8,128)(2,1)S(1)}, bf16[2,1,128,2048]{3,2,1,0:T(8,128)(2,1)}, u32[]{:S(2)}) copy-start(bf16[2,1,128,2048]{3,2,1,0:T(8,128)(2,1)} %param.17) | copy-start | bytes 3145732
  637.3 108.5 %copy-start.62 = (f32[2048]{0:T(1024)S(1)}, f32[2048]{0:T(1024)}, u32[]{:S(2)}) copy-start(f32[2048]{0:T(1024)} %param.18) | copy-start | bytes 24580
  637.4 108.5 %copy-start.99 = (f32[128]{0:T(128)S(1)}, f32[128]{0:T(128)}, u32[]{:S(2)}) copy-start(f32[128]{0:T(128)} %copy-done.98) | copy-start | bytes 1540
  637.4 406.7 %reduce-scatter.23.cloned.1.call-start = ((), (), s32[]{:S(2)}) async-start(), calls=%async_computation.29 | async-start | bytes 2228224 | tf_op jit(solution)/shard_map/reduce_scatter | solution.py:242
  637.5 108.4 %copy-start.49 = (f32[128,256]{1,0:T(8,128)S(1)}, f32[128,256]{1,0:T(8,128)}, u32[]{:S(2)}) copy-start(f32[128,256]{1,0:T(8,128)} %reduce-scatter.15.cloned.1.call-done) | copy-start | bytes 393220
  640.3 107.6 %copy-start.111 = (f32[128]{0:T(128)S(1)}, f32[128]{0:T(128)}, u32[]{:S(2)}) copy-start(f32[128]{0:T(128)} %copy-done.110) | copy-start | bytes 1540
  640.3 214.5 %copy-start.44 = (bf16[2,1,128,2048]{3,2,1,0:T(8,128)(2,1)S(1)}, bf16[2,1,128,2048]{3,2,1,0:T(8,128)(2,1)}, u32[]{:S(2)}) copy-start(bf16[2,1,128,2048]{3,2,1,0:T(8,128)(2,1)} %param.33) | copy-start | bytes 3145732
  640.3 451.1 %all-gather.23.cloned.1.call-start = ((), (), s32[]{:S(2)}) async-start(), calls=%async_computation.22 | async-start | bytes 1572864 | tf_op jit(solution)/shard_map/all_gather | solution.py:257
  857.4 71.5 %copy-start.114 = (u32[32]{0:T(128)S(1)}, u32[32]{0:T(128)}, u32[]{:S(2)}) copy-start(u32[32]{0:T(128)} %constant.176) | copy-start | bytes 388
  899.7 23.1 %all-to-all-start.3 = ((bf16[8,128,256]{2,1,0:T(8,128)(2,1)}), bf16[8,128,256]{2,1,0:T(8,128)(2,1)S(1)}, u32[]{:S(2)}, u32[]{:S(2)}) async-start(bf16[8,128,256]{2,1,0:T(8,128)(2,1)} %bitcast.584), calls=%async_computation.7 | async-start | bytes 1048576 | tf_op jit(solution)/shard_map/all_to_all | solution.py:226
  905.7 185.6 %all-gather.25.cloned.1.call-start = ((), (), s32[]{:S(2)}) async-start(), calls=%async_computation.25 | async-start | bytes 3145728 | tf_op jit(solution)/shard_map/all_gather | solution.py:257
  905.7 47.7 %copy-start.107 = (f32[32]{0:T(128)S(1)}, f32[32]{0:T(128)}, u32[]{:S(2)}) copy-start(f32[32]{0:T(128)} %param.28) | copy-start | bytes 388
  905.7 47.7 %copy-start.109 = (f32[4]{0:T(128)S(1)}, f32[4]{0:T(128)}, u32[]{:S(2)}) copy-start(f32[4]{0:T(128)} %get-tuple-element.130) | copy-start | bytes 52
  922.8 24.5 %all-to-all-start.4 = ((bf16[8,128,256]{2,1,0:T(8,128)(2,1)}), bf16[8,128,256]{2,1,0:T(8,128)(2,1)S(1)}, u32[]{:S(2)}, u32[]{:S(2)}) async-start(bf16[8,128,256]{2,1,0:T(8,128)(2,1)} %bitcast.583), calls=%async_computation.9 | async-start | bytes 1048576 | tf_op jit(solution)/shard_map/all_to_all | solution.py:226
  947.3 99.0 %all-to-all-start.6 = ((bf16[256,8,128]{2,0,1:T(8,128)(2,1)}), bf16[256,8,128]{2,0,1:T(8,128)(2,1)S(1)}, u32[]{:S(2)}, u32[]{:S(2)}) async-start(bf16[256,8,128]{2,0,1:T(8,128)(2,1)} %copy_bitcast_fusion), calls=%async_computation.12 | async-start | bytes 1048576 | tf_op jit(solution)/shard_map/all_to_all | solution.py:248
  953.4 138.0 %all-reduce.57.cloned.1.call-start = ((), (), s32[]{:S(2)}) async-start(), calls=%async_computation.30 | async-start | bytes 262144 | tf_op jit(solution)/shard_map/psum | solution.py:243
  (74 other events, 294.3 us)
Sparse Core Ops, SparseCore 0:
  11.8 92.2 all-gather.10
  106.2 24.0 all-gather.12
  133.1 54.8 all-gather.14
  190.0 20.8 all-gather.20
  213.5 74.2 all-gather.18
  289.8 20.1 all-gather.16
  566.2 70.9 reduce-scatter.14
  641.8 103.9 reduce-scatter.12
  750.4 104.3 reduce-scatter.10
  857.6 18.9 reduce-scatter.24
  879.3 20.3 reduce-scatter.16
  902.5 20.3 reduce-scatter.18
  925.1 20.3 reduce-scatter.20
  948.2 76.7 reduce-scatter.22
  1026.4 14.1 all-gather.22
  1042.7 11.7 all-gather.24
  1056.8 19.0 all-reduce.56
where the time goes:
time: 1110 us; the launch traced here: 1100 us
  waiting for transfers between devices  377 us (34%)
  blocking collectives  291 us (26%)
  matrix products  176 us (16%)
  other arithmetic  145 us (13%)
  local copies, waits for them, and re-layouts  72 us (6%)
  starting transfers between devices  27.2 us (2%)
  between operations  16.4 us (1%)
    reduce_scatter x1, waiting for transfers between devices, body(): lax.psum_scatter(dot_f32(scaled, wo).astype(BF16), everyone, scatter_dime...  107 us
    reduce_scatter x1, waiting for transfers between devices, body(): lax.psum_scatter(part_normed.astype(BF16), everyone, scatter_dimension=0,...  105 us
    another operation x2, other arithmetic, mixer(): cum = jnp.cumsum(dt * -jnp.exp(a_log), axis=2)  95.2 us
    all_gather x1, waiting for transfers between devices, body(): cot = lax.all_gather(my_cot, everyone, axis=0, tiled=True)  76.9 us
    all_gather x3, blocking collectives, body(): lax.all_gather(a, 'seq', axis=a.ndim - 1, tiled=True)  62.8 us
    psum x1, blocking collectives, body(): lax.psum(jnp.stack([jnp.sum(gated * gated, axis=-1), jnp.sum(gs * gated,...  48.8 us
    psum x1, blocking collectives, body(): lax.psum((grad_norm, d_cbw, d_cbb), ('dp', 'seq', 'head'))  43.9 us
    all_gather x1, blocking collectives, body(): lax.all_gather(w_dt_in, ('dp', 'seq'), axis=0, tiled=True)  42.2 us
  transfers between devices with their start and end apart: 21, of which 9 were waited for; matrix products, arithmetic and copies ran while one was open for 16% of the time, Pallas kernels for 0%

commit v1 on v0

--- a/solution.py
+++ b/solution.py
@@ -8,6 +8,12 @@
 BF16 = jnp.bfloat16
 F32 = jnp.float32
 CHUNK = 128
+
+
+def rest_joints(vals, mesh_ax, a_name="dp"):
+    for h in (mesh_ax, a_name):
+        vals = jax.lax.psum(vals, axis_name=h)
+    return vals
 
 
 def dot_f32(a, b):
@@ -258,7 +264,7 @@
 
     small = lax.psum((d_cxw, d_cxb, d_dtb, d_alog, d_dsk, grad_gain), "dp")
     small = [lax.all_gather(a, "seq", axis=a.ndim - 1, tiled=True) for a in small]
-    grad_norm, d_cbw, d_cbb = lax.psum((grad_norm, d_cbw, d_cbb), ("dp", "seq", "head"))
+    grad_norm, d_cbw, d_cbb = rest_joints((grad_norm, d_cbw, d_cbb), ("seq", "head"))
     return (
         whole(result_own),
         whole(grad_own),

time: 1110 us -> 1210 us (1.090)
  waiting for transfers between devices: 377 us -> 449 us
  blocking collectives: 291 us -> 311 us
    reduce_scatter x1, waiting for transfers between devices: 0.02 us -> 71.1 us  [body(): lax.psum_scatter(lax.psum(weight_grad(normed_own, gb_own), 'head'), ('dp'...]
  transfers between devices with their start and end apart: 21 -> 21, of which waited for: 9 -> 10; matrix products, arithmetic and copies ran while one was open for 16% -> 14% of each run, Pallas kernels for 0% -> 0%
where the time goes in v1:
time: 1210 us; the launch traced here: 1200 us
  waiting for transfers between devices  449 us (37%)
  blocking collectives  311 us (26%)
  matrix products  176 us (15%)
  other arithmetic  145 us (12%)
  local copies, waits for them, and re-layouts  72 us (6%)
  starting transfers between devices  27.2 us (2%)
  between operations  16.4 us (1%)
    reduce_scatter x1, waiting for transfers between devices, body(): lax.psum_scatter(dot_f32(scaled, wo).astype(BF16), everyone, scatter_dime...  107 us
    reduce_scatter x1, waiting for transfers between devices, body(): lax.psum_scatter(part_normed.astype(BF16), everyone, scatter_dimension=0,...  106 us
    another operation x2, other arithmetic, mixer(): cum = jnp.cumsum(dt * -jnp.exp(a_log), axis=2)  95.2 us
    all_gather x1, waiting for transfers between devices, body(): cot = lax.all_gather(my_cot, everyone, axis=0, tiled=True)  76.9 us
    reduce_scatter x1, waiting for transfers between devices, body(): lax.psum_scatter(lax.psum(weight_grad(normed_own, gb_own), 'head'), ('dp'...  71.1 us
    all_gather x3, blocking collectives, body(): lax.all_gather(a, 'seq', axis=a.ndim - 1, tiled=True)  70.4 us
    psum x2, blocking collectives, rest_joints(): vals = jax.lax.psum(vals, axis_name=h)  61 us
    psum x1, blocking collectives, body(): lax.psum(jnp.stack([jnp.sum(gated * gated, axis=-1), jnp.sum(gs * gated,...  48.8 us
  transfers between devices with their start and end apart: 21, of which 10 were waited for; matrix products, arithmetic and copies ran while one was open for 14% of the time, Pallas kernels for 0%

profile of v1, /device:TPU:14, one launch (start us, length us, event | category | flops | bytes accessed | tf_op | source)
XLA Modules:
  0.0 1196.3 jit_solution(2877715779639987504)
XLA Ops:
  12.0 27.5 %all_to_all.115 = bf16[128,8,256]{0,2,1:T(8,128)(2,1)S(1)} all-to-all(bf16[128,8,256]{0,2,1:T(8,128)(2,1)S(1)} %bitcast.572), channel_id=1, replica_groups=mesh['dp'=2,'seq'=8,'head'=2] {'seq'}, dimensions={1} | all-to-all | bytes 1048576 | tf_op jit(solution)/shard_map/all_to_all | solution.py:145
  41.4 28.8 %all_to_all.116 = bf16[8,256,128]{2,1,0:T(8,128)(2,1)S(1)} all-to-all(bf16[8,256,128]{2,1,0:T(8,128)(2,1)S(1)} %bitcast.582), channel_id=1, replica_groups=mesh['dp'=2,'seq'=8,'head'=2] {'seq'}, dimensions={0} | all-to-all | bytes 1048576 | tf_op jit(solution)/shard_map/all_to_all | solution.py:158
  73.2 8.3 all-to-all-start.1
  83.4 42.2 %all_gather.47 = bf16[2048,32]{0,1:T(8,128)(2,1)S(1)} all-gather(bf16[128,32]{0,1:T(8,128)(2,1)S(1)} %copy-done.97), channel_id=1, replica_groups=mesh['dp'=2,'seq'=8,'head'=2] {'dp','seq'}, dimensions={0}, use_global_device_ids=true | all-gather | bytes 139264 | tf_op jit(solution)/shard_map/all_gather | solution.py:154
  129.6 5.6 fusion.19
  135.8 47.9 %fusion.184 = f32[2,8,128,4]{3,1,2,0:T(8,128)S(1)} fusion(f32[2,8,128,4]{3,1,2,0:T(8,128)S(1)} %copy.524), kind=kOutput, calls=%fused_computation.362 | output fusion | flops 1040384 | bytes 65536 | tf_op jit(solution)/shard_map/jvp(jit(cumsum))/reduce_window_sum | solution.py:47
  184.5 6.0 convolution_convert_fusion.6
  192.2 6.0 convolution_convert_fusion.5
  198.6 12.3 %all-gather.21.cloned.1.call-done = bf16[256,2048]{0,1:T(8,128)(2,1)} async-done(((bf16[256,1024]{0,1:T(8,128)(2,1)}), bf16[256,2048]{0,1:T(8,128)(2,1)}) %all-gather.21.cloned.1.call-update) | async-done | bytes 1048592 | tf_op jit(solution)/shard_map/all_gather | solution.py:157
  210.9 76.9 %all-gather.19.cloned.1.call-done = bf16[2048,2048]{1,0:T(8,128)(2,1)} async-done(((bf16[128,2048]{1,0:T(8,128)(2,1)}), bf16[2048,2048]{1,0:T(8,128)(2,1)}) %all-gather.19.cloned.1.call-update) | async-done | bytes 8388624 | tf_op jit(solution)/shard_map/all_gather | solution.py:163
  287.8 7.3 fusion.188
  295.1 3.0 copy.565
  298.3 11.7 all-gather.17.cloned.1.call-done
  310.0 6.0 convolution_convert_fusion.4
  318.4 2.9 copy.560
  321.4 6.9 fusion.44
  328.3 5.1 reshape.593
  333.3 4.9 copy.522
  338.3 2.6 fusion.43
  356.7 10.7 multiply_reduce_fusion.16
  367.4 3.1 copy.559
  370.5 2.6 multiply_reduce_fusion.15
  373.1 48.8 %psum.98 = f32[2,2,1024]{2,1,0:T(2,128)S(1)} all-reduce(f32[2,2,1024]{2,1,0:T(2,128)S(1)} %pad_maximum_fusion), channel_id=1, replica_groups=mesh['dp'=2,'seq'=8,'head'=2] {'seq','head'}, use_global_device_ids=true, to_apply=%region_4.5 | all-reduce | flops 4096 | bytes 32768 | tf_op jit(solution)/shard_map/psum | solution.py:194
  423.2 5.9 multiply_reduce_fusion.13
  429.2 3.6 fusion.72
  436.4 4.5 fusion.69
  440.9 3.3 fusion.111
  447.5 4.5 fusion.78
  452.0 3.2 fusion.51
  455.2 12.5 %fusion.12 = (f32[2,8,128,128]{3,2,1,0:T(8,128)}, f32[2,8,128,128,4]{3,2,4,1,0:T(8,128)}) fusion(f32[2,8,128,4]{2,3,1,0:T(4,128)S(1)} %copy-done.72, pred[2,8,128,128]{3,2,1,0:T(8,128)(4,1)S(1)} %copy-done.51, pred[8,128,128]{2,1,0:T(8,128)(4,1)S(1)} %copy-done.56, f32[2,8,128,128]{3,2,1,0:T(8,128)S(1)} %copy-done.41, ...), kind=kOutput, calls=%fused_computation.18 | convolution fusion | flops 824442880 | bytes 10944512 | tf_op jit(solution)/shard_map/transpose(jvp(sktuh,skuhp->skthp))/dot_general | solution.py:80
  467.7 4.6 fusion.90
  474.5 4.1 fusion.175
  478.7 9.8 multiply_reduce_fusion
  491.9 47.3 %fusion.185 = f32[2,8,128,4]{3,1,2,0:T(8,128)S(1)} fusion(f32[2,8,128,4]{3,1,2,0:T(8,128)S(1)} %copy.609), kind=kOutput, calls=%fused_computation.363 | output fusion | flops 1040384 | bytes 65536 | tf_op jit(solution)/shard_map/transpose(jvp(jit(cumsum)))/reduce_window_sum | solution.py:47
  539.8 4.8 copy.658
  544.6 5.8 reshape.594
  550.5 3.4 multiply_reduce_fusion.10
  566.2 8.1 fusion.156
  574.3 3.2 multiply_reduce_fusion.2
  577.5 8.4 fusion.189
  585.9 16.1 %add_convert_fusion = bf16[2048,2048]{1,0:T(8,128)(2,1)} fusion(f32[2048,2048]{1,0:T(8,128)} %fusion.156, f32[2048,2048]{1,0:T(8,128)} %fusion.189, bf16[2048,256]{1,0:T(8,128)(2,1)S(1)} %bitcast.562, bf16[2048,256]{1,0:T(8,128)(2,1)S(1)} %copy-done.36), kind=kOutput, calls=%fused_computation | convolution fusion | flops 2160066560 | bytes 44040192 | tf_op jit(solution)/shard_map/rc,kc->rk/dot_general | solution.py:218
  603.5 5.6 convolution_convert_fusion
  609.2 6.9 fusion.190
  616.4 6.9 convolution_convert_fusion.3
  623.4 7.0 convolution_convert_fusion.2
  630.4 6.9 convolution_convert_fusion.1
  637.5 2.8 fusion.150
  640.3 105.6 %reduce-scatter.13.cloned.1.call-done = bf16[128,2048]{1,0:T(8,128)(2,1)} async-done(((bf16[2048,2048]{1,0:T(8,128)(2,1)}), bf16[128,2048]{1,0:T(8,128)(2,1)}) %reduce-scatter.13.cloned.1.call-update) | async-done | bytes 524304 | tf_op jit(solution)/shard_map/reduce_scatter | solution.py:224
  748.0 107.0 %reduce-scatter.11.cloned.1.call-done = bf16[128,2048]{1,0:T(8,128)(2,1)} async-done(((bf16[2048,2048]{1,0:T(8,128)(2,1)}), bf16[128,2048]{1,0:T(8,128)(2,1)}) %reduce-scatter.11.cloned.1.call-update) | async-done | bytes 524304 | tf_op jit(solution)/shard_map/reduce_scatter | solution.py:200
  857.6 19.1 %reduce-scatter.25.cloned.1.call-done = f32[1024,4]{1,0:T(8,128)} async-done(((f32[2048,4]{1,0:T(8,128)}), f32[1024,4]{1,0:T(8,128)}) %reduce-scatter.25.cloned.1.call-update) | async-done | bytes 16400
  878.0 10.1 all_to_all.117
  888.0 11.8 reduce-scatter.17.cloned.1.call-done
  899.9 6.0 all-to-all-start.3
  906.5 16.5 %reduce-scatter.19.cloned.1.call-done = bf16[1024,256]{1,0:T(8,128)(2,1)} async-done(((bf16[2048,256]{1,0:T(8,128)(2,1)}), bf16[1024,256]{1,0:T(8,128)(2,1)}) %reduce-scatter.19.cloned.1.call-update) | async-done | bytes 524304 | tf_op jit(solution)/shard_map/reduce_scatter | solution.py:233
  923.0 6.0 all-to-all-start.4
  930.3 15.3 %reduce-scatter.21.cloned.1.call-done = bf16[256,1024]{1,0:T(8,128)(2,1)} async-done(((bf16[256,2048]{1,0:T(8,128)(2,1)}), bf16[256,1024]{1,0:T(8,128)(2,1)}) %reduce-scatter.21.cloned.1.call-update) | async-done | bytes 524304 | tf_op jit(solution)/shard_map/reduce_scatter | solution.py:255
  947.5 6.0 all-to-all-start.6
  954.0 71.1 %reduce-scatter.23.cloned.1.call-done = f32[128,256]{1,0:T(8,128)} async-done(((f32[2048,256]{1,0:T(8,128)}), f32[128,256]{1,0:T(8,128)}) %reduce-scatter.23.cloned.1.call-update) | async-done | bytes 131088 | tf_op jit(solution)/shard_map/reduce_scatter | solution.py:248
  1028.4 53.1 %all-reduce.52 = (f32[2048]{0:T(1024)S(1)}, f32[4,256]{1,0:T(4,128)S(1)}, f32[256]{0:T(256)S(1)}) all-reduce(f32[2048]{0:T(1024)S(1)} %get-tuple-element.135, f32[4,256]{1,0:T(4,128)S(1)} %pad_add_fusion.10, f32[256]{0:T(256)S(1)} %get-tuple-element.131), channel_id=1, replica_groups=mesh['dp'=2,'seq'=8,'head'=2] {'seq','head'}, use_global_device_ids=true, to_apply=%region_33.34 | all-reduce | flops 3328 | bytes 26624 | tf_op jit(solution)/shard_map/psum | solution.py:15
  1081.5 7.9 all-reduce.54
  1089.4 26.4 %all-gather = f32[8,1,256]{2,1,0:T(1,128)S(1)} all-gather(f32[1,1,256]{2,1,0:T(1,128)S(1)} %bitcast.633), channel_id=1, replica_groups=mesh['dp'=2,'seq'=8,'head'=2] {'seq'}, dimensions={0}, use_global_device_ids=true | all-gather | bytes 9216 | tf_op jit(solution)/shard_map/all_gather | solution.py:266
  1115.8 16.3 %all-gather.1 = f32[8,1,256]{2,1,0:T(1,128)S(1)} all-gather(f32[1,1,256]{2,1,0:T(1,128)S(1)} %bitcast.632), channel_id=1, replica_groups=mesh['dp'=2,'seq'=8,'head'=2] {'seq'}, dimensions={0}, use_global_device_ids=true | all-gather | bytes 9216 | tf_op jit(solution)/shard_map/all_gather | solution.py:266
  1132.1 27.7 %all_gather.54 = f32[4,2048]{1,0:T(4,128)S(1)} all-gather(f32[4,256]{1,0:T(4,128)S(1)} %get-tuple-element.165), channel_id=1, replica_groups=mesh['dp'=2,'seq'=8,'head'=2] {'seq'}, dimensions={1}, use_global_device_ids=true | all-gather | bytes 36864 | tf_op jit(solution)/shard_map/all_gather | solution.py:266
  1160.4 22.3 %all-reduce.53 = (f32[32]{0:T(128)}, f32[32]{0:T(128)}, f32[32]{0:T(128)}) all-reduce(f32[32]{0:T(128)S(1)} %dynamic-update-slice, f32[32]{0:T(128)S(1)} %dynamic-update-slice.1, f32[32]{0:T(128)S(1)} %dynamic-update-slice.2), channel_id=1, replica_groups=mesh['dp'=2,'seq'=8,'head'=2] {'seq'}, use_global_device_ids=true, to_apply=%add.49 | all-reduce | flops 96 | bytes 768
  (405 shorter events, 85.4 us)
Async XLA Ops:
  7.2 122.4 %all-gather.11.cloned.1.call-start = ((), (), s32[]{:S(2)}) async-start(), calls=%async_computation.15 | async-start | bytes 8912896 | tf_op jit(solution)/shard_map/all_gather | solution.py:141
  11.7 29.7 %copy-start.47 = (bf16[2048,128]{1,0:T(8,128)(2,1)S(1)}, bf16[2048,128]{1,0:T(8,128)(2,1)}, u32[]{:S(2)}) copy-start(bf16[2048,128]{1,0:T(8,128)(2,1)} %param.31) | copy-start | bytes 1572868
  11.7 172.8 %all-gather.13.cloned.1.call-start = ((), (), s32[]{:S(2)}) async-start(), calls=%async_computation.16 | async-start | bytes 1572864 | tf_op jit(solution)/shard_map/all_gather | solution.py:144
  39.5 31.8 %copy-start.43 = (bf16[2,1,128,2048]{3,2,1,0:T(8,128)(2,1)S(1)}, bf16[2,1,128,2048]{3,2,1,0:T(8,128)(2,1)}, u32[]{:S(2)}) copy-start(bf16[2,1,128,2048]{3,2,1,0:T(8,128)(2,1)} %param.33) | copy-start | bytes 3145732
  40.6 151.7 %all-gather.15.cloned.1.call-start = ((), (), s32[]{:S(2)}) async-start(), calls=%async_computation.17 | async-start | bytes 1114112 | tf_op jit(solution)/shard_map/all_gather | solution.py:156
  41.3 169.6 %all-gather.21.cloned.1.call-start = ((), (), s32[]{:S(2)}) async-start(), calls=%async_computation.20 | async-start | bytes 1572864 | tf_op jit(solution)/shard_map/all_gather | solution.py:157
  41.4 30.9 %copy-start.48 = (bf16[128,2048]{1,0:T(8,128)(2,1)S(1)}, bf16[128,2048]{1,0:T(8,128)(2,1)}, u32[]{:S(2)}) copy-start(bf16[128,2048]{1,0:T(8,128)(2,1)} %param.19) | copy-start | bytes 1572868
  71.2 12.1 %copy-start.97 = (bf16[128,32]{0,1:T(8,128)(2,1)S(1)}, bf16[128,32]{0,1:T(8,128)(2,1)}, u32[]{:S(2)}) copy-start(bf16[128,32]{0,1:T(8,128)(2,1)} %param.22) | copy-start | bytes 24580
  71.3 54.3 %copy-start.112 = (f32[32]{0:T(128)S(1)}, f32[32]{0:T(128)}, u32[]{:S(2)}) copy-start(f32[32]{0:T(128)} %param.27) | copy-start | bytes 388
  71.3 54.4 %copy-start.113 = (f32[32]{0:T(128)S(1)}, f32[32]{0:T(128)}, u32[]{:S(2)}) copy-start(f32[32]{0:T(128)} %param.29) | copy-start | bytes 388
  71.3 56.6 %copy-start.108 = (s32[2,1]{0,1:T(1,128)S(1)}, s32[2,1]{0,1:T(1,128)}, u32[]{:S(2)}) copy-start(s32[2,1]{0,1:T(1,128)} %param.32) | copy-start | bytes 28
  71.3 56.7 %copy-start.104 = (f32[4,256]{1,0:T(4,128)S(1)}, f32[4,256]{1,0:T(4,128)}, u32[]{:S(2)}) copy-start(f32[4,256]{1,0:T(4,128)} %param.25) | copy-start | bytes 12292
  71.3 216.5 %all-gather.19.cloned.1.call-start = ((), (), s32[]{:S(2)}) async-start(), calls=%async_computation.19 | async-start | bytes 8912896 | tf_op jit(solution)/shard_map/all_gather | solution.py:163
  73.2 55.2 %all-to-all-start.1 = ((bf16[128,8,256]{0,2,1:T(8,128)(2,1)}), bf16[128,8,256]{0,2,1:T(8,128)(2,1)S(1)}, u32[]{:S(2)}, u32[]{:S(2)}) async-start(bf16[128,8,256]{0,2,1:T(8,128)(2,1)} %bitcast.42), calls=%async_computation.1 | async-start | bytes 1048576 | tf_op jit(solution)/shard_map/all_to_all | solution.py:145
  81.6 228.4 %all-gather.17.cloned.1.call-start = ((), (), s32[]{:S(2)}) async-start(), calls=%async_computation.18 | async-start | bytes 1572864 | tf_op jit(solution)/shard_map/all_gather | solution.py:144
  81.7 53.6 %copy-start.100 = (f32[4]{0:T(128)}, f32[4]{0:T(128)S(1)}, u32[]{:S(2)}) copy-start(f32[4]{0:T(128)S(1)} %fusion.174) | copy-start | bytes 52
  82.6 238.7 %copy-start.81 = (f32[1,256]{1,0:T(1,128)}, f32[1,256]{1,0:T(1,128)S(1)}, u32[]{:S(2)}) copy-start(f32[1,256]{1,0:T(1,128)S(1)} %get-tuple-element.233) | copy-start | bytes 3076
  82.6 238.7 %copy-start.83 = (f32[1,256]{1,0:T(1,128)}, f32[1,256]{1,0:T(1,128)S(1)}, u32[]{:S(2)}) copy-start(f32[1,256]{1,0:T(1,128)S(1)} %get-tuple-element.234) | copy-start | bytes 3076
  82.6 238.7 %copy-start.85 = (f32[1,256]{1,0:T(1,128)}, f32[1,256]{1,0:T(1,128)S(1)}, u32[]{:S(2)}) copy-start(f32[1,256]{1,0:T(1,128)S(1)} %get-tuple-element.235) | copy-start | bytes 3076
  82.6 238.7 %copy-start.87 = (f32[1,256]{1,0:T(1,128)}, f32[1,256]{1,0:T(1,128)S(1)}, u32[]{:S(2)}) copy-start(f32[1,256]{1,0:T(1,128)S(1)} %get-tuple-element.236) | copy-start | bytes 3076
  125.7 230.9 %copy-start.115 = (f32[4]{0:T(128)}, f32[4]{0:T(128)S(1)}, u32[]{:S(2)}) copy-start(f32[4]{0:T(128)S(1)} %dynamic_slice.33) | copy-start | bytes 52
  128.0 70.2 %copy-start.67 = (pred[2,8,128]{2,1,0:T(8,128)(4,1)}, pred[2,8,128]{2,1,0:T(8,128)(4,1)S(1)}, u32[]{:S(2)}) copy-start(pred[2,8,128]{2,1,0:T(8,128)(4,1)S(1)} %broadcast_compare_fusion.2) | copy-start | bytes 6148
  128.0 210.3 %copy-start.89 = (f32[1,256]{1,0:T(1,128)}, f32[1,256]{1,0:T(1,128)S(1)}, u32[]{:S(2)}) copy-start(f32[1,256]{1,0:T(1,128)S(1)} %get-tuple-element.242) | copy-start | bytes 3076
  128.0 210.3 %copy-start.91 = (f32[1,256]{1,0:T(1,128)}, f32[1,256]{1,0:T(1,128)S(1)}, u32[]{:S(2)}) copy-start(f32[1,256]{1,0:T(1,128)S(1)} %get-tuple-element.243) | copy-start | bytes 3076
  128.0 210.3 %copy-start.93 = (f32[1,256]{1,0:T(1,128)}, f32[1,256]{1,0:T(1,128)S(1)}, u32[]{:S(2)}) copy-start(f32[1,256]{1,0:T(1,128)S(1)} %get-tuple-element.244) | copy-start | bytes 3076
  128.0 210.3 %copy-start.95 = (f32[1,256]{1,0:T(1,128)}, f32[1,256]{1,0:T(1,128)S(1)}, u32[]{:S(2)}) copy-start(f32[1,256]{1,0:T(1,128)S(1)} %get-tuple-element.245) | copy-start | bytes 3076
  128.3 228.4 %copy-start.55 = (pred[8,128,128]{2,1,0:T(8,128)(4,1)}, pred[8,128,128]{2,1,0:T(8,128)(4,1)S(1)}, u32[]{:S(2)}) copy-start(pred[8,128,128]{2,1,0:T(8,128)(4,1)S(1)} %get-tuple-element.240) | copy-start | bytes 393220
  128.4 228.2 %copy-start.50 = (pred[2,8,128,128]{3,2,1,0:T(8,128)(4,1)}, pred[2,8,128,128]{3,2,1,0:T(8,128)(4,1)S(1)}, u32[]{:S(2)}) copy-start(pred[2,8,128,128]{3,2,1,0:T(8,128)(4,1)S(1)} %broadcast_and_fusion) | copy-start | bytes 786436
  129.5 508.0 %reduce-scatter.15.cloned.1.call-start = ((), (), s32[]{:S(2)}) async-start(), calls=%async_computation.24 | async-start | bytes 2228224 | tf_op jit(solution)/shard_map/reduce_scatter | solution.py:213
  184.5 172.2 %copy-start.71 = (f32[2,8,128,4]{2,3,1,0:T(4,128)}, f32[2,8,128,4]{2,3,1,0:T(4,128)S(1)}, u32[]{:S(2)}) copy-start(f32[2,8,128,4]{2,3,1,0:T(4,128)S(1)} %copy.525) | copy-start | bytes 98308
  198.4 148.2 %copy-start.59 = (f32[2,8,128,4]{2,3,1,0:T(4,128)}, f32[2,8,128,4]{2,3,1,0:T(4,128)S(1)}, u32[]{:S(2)}) copy-start(f32[2,8,128,4]{2,3,1,0:T(4,128)S(1)} %copy.546) | copy-start | bytes 98308
  198.6 139.7 %copy-start = (f32[8,2,128,256]{3,2,0,1:T(8,128)}, f32[8,2,128,256]{3,2,0,1:T(8,128)S(1)}, u32[]{:S(2)}) copy-start(f32[8,2,128,256]{3,2,0,1:T(8,128)S(1)} %copy.523) | copy-start | bytes 6291460
  298.3 47.0 %copy-start.76 = (f32[2,4]{1,0:T(2,128)}, f32[2,4]{1,0:T(2,128)S(1)}, u32[]{:S(2)}) copy-start(f32[2,4]{1,0:T(2,128)S(1)} %get-tuple-element.150) | copy-start | bytes 100
  298.3 50.6 %copy-start.63 = (f32[2,4]{1,0:T(2,128)}, f32[2,4]{1,0:T(2,128)S(1)}, u32[]{:S(2)}) copy-start(f32[2,4]{1,0:T(2,128)S(1)} %get-tuple-element.154) | copy-start | bytes 100
  298.3 50.6 %copy-start.65 = (f32[2,4]{1,0:T(2,128)}, f32[2,4]{1,0:T(2,128)S(1)}, u32[]{:S(2)}) copy-start(f32[2,4]{1,0:T(2,128)S(1)} %get-tuple-element.157) | copy-start | bytes 100
  298.3 51.1 %copy-start.74 = (f32[2,4]{1,0:T(2,128)}, f32[2,4]{1,0:T(2,128)S(1)}, u32[]{:S(2)}) copy-start(f32[2,4]{1,0:T(2,128)S(1)} %get-tuple-element.151) | copy-start | bytes 100
  341.1 13.2 %copy-start.3 = (f32[2,1024,128]{2,1,0:T(8,128)}, f32[2,1024,128]{2,1,0:T(8,128)S(1)}, u32[]{:S(2)}) copy-start(f32[2,1024,128]{2,1,0:T(8,128)S(1)} %get-tuple-element.224) | copy-start | bytes 3145732
  354.2 13.1 %copy-start.27 = (f32[2,8,128,4,64]{2,4,3,1,0:T(8,128)}, f32[2,8,128,4,64]{2,4,3,1,0:T(8,128)S(1)}, u32[]{:S(2)}) copy-start(f32[2,8,128,4,64]{2,4,3,1,0:T(8,128)S(1)} %fusion.55) | copy-start | bytes 6291460
  455.2 12.5 %copy-start.20 = (f32[2,8,4,64,128]{4,3,2,0,1:T(8,128)S(1)}, f32[2,8,4,64,128]{4,3,2,0,1:T(8,128)}, u32[]{:S(2)}) copy-start(f32[2,8,4,64,128]{4,3,2,0,1:T(8,128)} %copy-done.19) | copy-start | bytes 6291460
  491.5 48.1 %copy-start.53 = (f32[2,8,128,4]{2,3,1,0:T(4,128)S(1)}, f32[2,8,128,4]{2,3,1,0:T(4,128)}, u32[]{:S(2)}) copy-start(f32[2,8,128,4]{2,3,1,0:T(4,128)} %get-tuple-element.137) | copy-start | bytes 98308
  491.5 48.1 %copy-start.101 = (f32[4]{0:T(128)S(1)}, f32[4]{0:T(128)}, u32[]{:S(2)}) copy-start(f32[4]{0:T(128)} %copy-done.100) | copy-start | bytes 52
  491.5 48.1 %copy-start.103 = (f32[4]{0:T(128)S(1)}, f32[4]{0:T(128)}, u32[]{:S(2)}) copy-start(f32[4]{0:T(128)} %copy-done.102) | copy-start | bytes 52
  566.1 179.8 %reduce-scatter.13.cloned.1.call-start = ((), (), s32[]{:S(2)}) async-start(), calls=%async_computation.23 | async-start | bytes 8912896 | tf_op jit(solution)/shard_map/reduce_scatter | solution.py:224
  602.0 253.0 %reduce-scatter.11.cloned.1.call-start = ((), (), s32[]{:S(2)}) async-start(), calls=%async_computation.21 | async-start | bytes 8912896 | tf_op jit(solution)/shard_map/reduce_scatter | solution.py:200
  609.1 267.6 %reduce-scatter.25.cloned.1.call-start = ((), (), s32[]{:S(2)}) async-start(), calls=%async_computation.31 | async-start | bytes 1572864
  616.1 283.8 %reduce-scatter.17.cloned.1.call-start = ((), (), s32[]{:S(2)}) async-start(), calls=%async_computation.26 | async-start | bytes 1572864 | tf_op jit(solution)/shard_map/reduce_scatter | solution.py:233
  623.3 299.7 %reduce-scatter.19.cloned.1.call-start = ((), (), s32[]{:S(2)}) async-start(), calls=%async_computation.27 | async-start | bytes 1572864 | tf_op jit(solution)/shard_map/reduce_scatter | solution.py:233
  630.4 315.2 %reduce-scatter.21.cloned.1.call-start = ((), (), s32[]{:S(2)}) async-start(), calls=%async_computation.28 | async-start | bytes 1572864 | tf_op jit(solution)/shard_map/reduce_scatter | solution.py:255
  637.3 108.6 %copy-start.31 = (bf16[2,1,128,2048]{3,2,1,0:T(8,128)(2,1)S(1)}, bf16[2,1,128,2048]{3,2,1,0:T(8,128)(2,1)}, u32[]{:S(2)}) copy-start(bf16[2,1,128,2048]{3,2,1,0:T(8,128)(2,1)} %param.17) | copy-start | bytes 3145732
  637.3 108.5 %copy-start.62 = (f32[2048]{0:T(1024)S(1)}, f32[2048]{0:T(1024)}, u32[]{:S(2)}) copy-start(f32[2048]{0:T(1024)} %param.18) | copy-start | bytes 24580
  637.4 108.5 %copy-start.99 = (f32[128]{0:T(128)S(1)}, f32[128]{0:T(128)}, u32[]{:S(2)}) copy-start(f32[128]{0:T(128)} %copy-done.98) | copy-start | bytes 1540
  637.4 387.7 %reduce-scatter.23.cloned.1.call-start = ((), (), s32[]{:S(2)}) async-start(), calls=%async_computation.29 | async-start | bytes 2228224 | tf_op jit(solution)/shard_map/reduce_scatter | solution.py:248
  637.5 108.4 %copy-start.49 = (f32[128,256]{1,0:T(8,128)S(1)}, f32[128,256]{1,0:T(8,128)}, u32[]{:S(2)}) copy-start(f32[128,256]{1,0:T(8,128)} %reduce-scatter.15.cloned.1.call-done) | copy-start | bytes 393220
  640.3 107.7 %copy-start.111 = (f32[128]{0:T(128)S(1)}, f32[128]{0:T(128)}, u32[]{:S(2)}) copy-start(f32[128]{0:T(128)} %copy-done.110) | copy-start | bytes 1540
  640.3 214.7 %copy-start.44 = (bf16[2,1,128,2048]{3,2,1,0:T(8,128)(2,1)S(1)}, bf16[2,1,128,2048]{3,2,1,0:T(8,128)(2,1)}, u32[]{:S(2)}) copy-start(bf16[2,1,128,2048]{3,2,1,0:T(8,128)(2,1)} %param.33) | copy-start | bytes 3145732
  640.3 542.4 %all-gather.23.cloned.1.call-start = ((), (), s32[]{:S(2)}) async-start(), calls=%async_computation.22 | async-start | bytes 1572864 | tf_op jit(solution)/shard_map/all_gather | solution.py:263
  857.6 71.4 %copy-start.114 = (u32[32]{0:T(128)S(1)}, u32[32]{0:T(128)}, u32[]{:S(2)}) copy-start(u32[32]{0:T(128)} %constant.176) | copy-start | bytes 388
  899.9 23.1 %all-to-all-start.3 = ((bf16[8,128,256]{2,1,0:T(8,128)(2,1)}), bf16[8,128,256]{2,1,0:T(8,128)(2,1)S(1)}, u32[]{:S(2)}, u32[]{:S(2)}) async-start(bf16[8,128,256]{2,1,0:T(8,128)(2,1)} %bitcast.584), calls=%async_computation.7 | async-start | bytes 1048576 | tf_op jit(solution)/shard_map/all_to_all | solution.py:232
  905.9 276.8 %all-gather.25.cloned.1.call-start = ((), (), s32[]{:S(2)}) async-start(), calls=%async_computation.25 | async-start | bytes 3145728 | tf_op jit(solution)/shard_map/all_gather | solution.py:263
  905.9 47.9 %copy-start.107 = (f32[32]{0:T(128)S(1)}, f32[32]{0:T(128)}, u32[]{:S(2)}) copy-start(f32[32]{0:T(128)} %param.28) | copy-start | bytes 388
  923.0 24.5 %all-to-all-start.4 = ((bf16[8,128,256]{2,1,0:T(8,128)(2,1)}), bf16[8,128,256]{2,1,0:T(8,128)(2,1)S(1)}, u32[]{:S(2)}, u32[]{:S(2)}) async-start(bf16[8,128,256]{2,1,0:T(8,128)(2,1)} %bitcast.583), calls=%async_computation.9 | async-start | bytes 1048576 | tf_op jit(solution)/shard_map/all_to_all | solution.py:232
  947.5 79.8 %all-to-all-start.6 = ((bf16[256,8,128]{2,0,1:T(8,128)(2,1)}), bf16[256,8,128]{2,0,1:T(8,128)(2,1)S(1)}, u32[]{:S(2)}, u32[]{:S(2)}) async-start(bf16[256,8,128]{2,0,1:T(8,128)(2,1)} %copy_bitcast_fusion), calls=%async_computation.12 | async-start | bytes 1048576 | tf_op jit(solution)/shard_map/all_to_all | solution.py:254
  953.5 229.2 %all-reduce.57.cloned.1.call-start = ((), (), s32[]{:S(2)}) async-start(), calls=%async_computation.30 | async-start | bytes 262144 | tf_op jit(solution)/shard_map/psum | solution.py:249
  1026.3 55.2 %copy-start.109 = (f32[4]{0:T(128)S(1)}, f32[4]{0:T(128)}, u32[]{:S(2)}) copy-start(f32[4]{0:T(128)} %get-tuple-element.130) | copy-start | bytes 52
  (74 other events, 294.3 us)
Sparse Core Ops, SparseCore 0:
  11.8 92.2 all-gather.10
  106.2 24.0 all-gather.12
  133.1 54.8 all-gather.14
  190.0 20.8 all-gather.20
  213.5 74.2 all-gather.18
  289.8 20.1 all-gather.16
  566.2 70.9 reduce-scatter.14
  641.8 104.0 reduce-scatter.12
  750.5 104.4 reduce-scatter.10
  857.7 18.9 reduce-scatter.24
  879.5 20.2 reduce-scatter.16
  902.6 20.3 reduce-scatter.18
  925.2 20.3 reduce-scatter.20
  948.4 76.6 reduce-scatter.22
  1026.5 14.3 all-gather.22
  1042.9 11.7 all-gather.24
  1057.0 19.0 all-reduce.56
